TPU v7x, 128 devices: a whole 4x4x4 slice. The times are simulated.
128 devices in a mesh: corpus: 32 (over y, z, core), tensor: 4 (over x).
Axes of the slice: x: 4, y: 4, z: 4, core: 2. Of those that a mesh axis runs over, the one named last changes fastest.
Arguments:
- hidden: bfloat16 [12288, 4096], P('corpus', 'tensor'), may hold values from -6 to 6
- lengths: int32 [32, 32], P('corpus'), may hold values from 1 to 48, 384 in all within a row
- steer_ids: int32 [1024], P('corpus'), may hold values from 0 to 15
- in_gain: float32 [4096], replicated, may hold values from 0.6 to 14
- w_query: bfloat16 [4096, 2048], P(None, 'tensor'), may hold values from -0.09375 to 0.09375
- w_key: bfloat16 [4096, 1024], P(None, 'tensor'), may hold values from -0.09375 to 0.09375
- w_value: bfloat16 [4096, 1024], P(None, 'tensor'), may hold values from -0.09375 to 0.09375
- w_out: bfloat16 [2048, 4096], P('tensor'), may hold values from -0.125 to 0.125
- steer_table: bfloat16 [16, 4096], replicated, may hold values from -12 to 12
- strength: float32 [16], replicated, may hold values from 0.1 to 0.5
- out_gain: float32 [4096], replicated, may hold values from 0.1 to 1.9
- index_rows: bfloat16 [131072, 4096], P(('corpus', 'tensor')), may hold values from -6 to 6
Outputs:
- scores: bfloat16 [1024, 131072], P(None, ('corpus', 'tensor'))
Inputs may be any that keep to these rules, and one draw needn't show every extreme that they name: Each row of lengths holds the token counts of the 32 queries packed in order into the 384 tokens of one group.
All inputs are finite; a program needn't handle non-finite values.
Results may differ from a plain program's by a relative error of at most 0.005.
The roundings to bfloat16 on the way count: a program that leaves them out, or rounds other values in their place, can miss the bound.
Values may be sent and summed in bfloat16 or wider, within the bound.
No kernel may reach another device: no remote copies, remote signals or barrier semaphores. Data moves between devices by JAX's collectives and lax.ppermute only.
A program may use at most 128 MiB of HBM per device.

v0:
```python
import jax
import jax.numpy as jnp
from jax import lax
from jax.sharding import PartitionSpec as P

D = 4096
HEAD = 128
rope_base = 1000000.0


def rotate(vectors, positions):
    half_width = vectors.shape[-1] // 2
    frequency = rope_base ** (
        -(jnp.arange(half_width, dtype=jnp.float32) * 2.0) / vectors.shape[-1]
    )
    angles = positions.astype(jnp.float32)[:, None] * frequency[None, :]
    cosine = jnp.cos(angles)[:, None, :]
    sine_part = jnp.sin(angles)[:, None, :]
    leading = vectors[..., :half_width]
    second = vectors[..., half_width:]
    return jnp.concatenate(
        [leading * cosine - second * sine_part, second * cosine + leading * sine_part], axis=-1
    )


def encode(normed, lengths_row, w_query, w_key, w_value):
    tok_count = normed.shape[0]
    query_count = lengths_row.shape[0]
    seq_ends = jnp.cumsum(lengths_row)
    starts = seq_ends - lengths_row
    places = jnp.arange(tok_count, dtype=jnp.int32)
    owners = jnp.sum((places[:, None] >= seq_ends[None, :]).astype(jnp.int32), axis=1)
    positions = places - jnp.take(starts, owners)
    finals = seq_ends - 1
    pooled = jnp.take(normed, finals, axis=0)
    kv_heads = w_key.shape[1] // HEAD
    q_heads = w_query.shape[1] // HEAD
    group_size = q_heads // kv_heads
    key_rows = jnp.dot(normed, w_key, preferred_element_type=jnp.float32).reshape(
        tok_count, kv_heads, HEAD
    )
    key_rows = rotate(key_rows, positions).astype(jnp.bfloat16)
    values = (
        jnp.dot(normed, w_value, preferred_element_type=jnp.float32)
        .astype(jnp.bfloat16)
        .reshape(tok_count, kv_heads, HEAD)
    )
    queries = jnp.dot(pooled, w_query, preferred_element_type=jnp.float32).reshape(
        query_count, q_heads, HEAD
    )
    queries = (
        rotate(queries, lengths_row - 1)
        .astype(jnp.bfloat16)
        .reshape(query_count, kv_heads, group_size, HEAD)
    )
    scores = jnp.einsum(
        "qgrd,tgd->grqt", queries, key_rows, preferred_element_type=jnp.float32
    ) * HEAD ** (-0.5)
    visible = (
        owners[None, None, None, :] == jnp.arange(query_count, dtype=jnp.int32)[None, None, :, None]
    )
    scores = jnp.where(visible, scores, -1e30)
    maxima = jnp.max(scores, axis=3, keepdims=True)
    weights = jnp.exp(scores - maxima)
    attn_probs = (weights / jnp.sum(weights, axis=3, keepdims=True)).astype(jnp.bfloat16)
    context = jnp.einsum("grqt,tgd->qgrd", attn_probs, values, preferred_element_type=jnp.float32)
    context = context.astype(jnp.bfloat16).reshape(query_count, q_heads * HEAD)
    return (context, finals)


def on_device(
    hidden,
    lengths,
    steer_ids,
    in_gain,
    w_query,
    w_key,
    w_value,
    w_out,
    steer_table,
    strength,
    out_gain,
    index_rows,
):
    group_rows = lax.all_gather(hidden, "tensor", axis=1, tiled=True)
    widened = group_rows.astype(jnp.float32)
    normed = (
        widened
        * lax.rsqrt(jnp.mean(widened * widened, axis=1, keepdims=True) + 1e-06)
        * in_gain[None, :]
    ).astype(jnp.bfloat16)
    context, finals = encode(normed, lengths[0], w_query, w_key, w_value)
    pooled_x = jnp.take(widened, finals, axis=0)
    one_hot = steer_ids[:, None] == jnp.arange(steer_table.shape[0], dtype=jnp.int32)[None, :]
    steering = jnp.dot(
        one_hot.astype(jnp.bfloat16), steer_table, preferred_element_type=jnp.float32
    )
    scaled = jnp.sum(jnp.where(one_hot, strength[None, :], 0.0), axis=1)
    partial_value = jnp.dot(context, w_out, preferred_element_type=jnp.float32)
    attn_out = lax.psum_scatter(partial_value, "tensor", scatter_dimension=1, tiled=True)
    local_width = attn_out.shape[1]
    column_start = lax.axis_index("tensor") * local_width
    residual = lax.dynamic_slice_in_dim(pooled_x, column_start, local_width, 1) + attn_out
    my_steering = lax.dynamic_slice_in_dim(steering, column_start, local_width, 1)
    my_gain = lax.dynamic_slice_in_dim(out_gain, column_start, local_width, 0)
    self_sq, steer_sq = lax.psum(
        (jnp.sum(residual * residual, axis=1), jnp.sum(my_steering * my_steering, axis=1)), "tensor"
    )
    factor = scaled * jnp.sqrt(self_sq / D / (steer_sq / D + 1e-06))
    gained = (residual + factor[:, None] * my_steering) * my_gain[None, :]
    totals = lax.psum(jnp.sum(gained * gained, axis=1), "tensor")
    local_embed = (gained * lax.rsqrt(totals + 1e-06)[:, None]).astype(jnp.bfloat16)
    embeddings = lax.all_gather(local_embed, "tensor", axis=1, tiled=True)
    return lax.dot_general(
        lax.all_gather(embeddings, "corpus", axis=0, tiled=True),
        index_rows,
        (((1,), (1,)), ((), ())),
        preferred_element_type=jnp.float32,
    ).astype(jnp.bfloat16)


def solution(mesh):
    placed = (
        P("corpus", "tensor"),
        P("corpus", None),
        P("corpus"),
        P(),
        P(None, "tensor"),
        P(None, "tensor"),
        P(None, "tensor"),
        P("tensor", None),
        P(),
        P(),
        P(),
        P(("corpus", "tensor"), None),
    )
    return jax.shard_map(
        on_device,
        mesh=mesh,
        in_specs=placed,
        out_specs=P(None, ("corpus", "tensor")),
        check_vma=False,
    )
```

profile of v0, /device:TPU:1, one launch (start us, length us, event | category | flops | bytes accessed | tf_op | source)
XLA Modules:
  0.0 206.8 jit_solution(14262951301222223644)
XLA Ops:
  6.5 0.7 all-gather.3.cloned.1.call-update
  7.3 0.0 reduce-scatter.2.cloned.1.call-start
  7.3 0.7 copy.26
  8.0 0.1 reduce-window.4
  8.1 0.1 fusion.23
  8.2 0.7 fusion.29
  8.9 0.7 fusion.49
  9.6 0.1 convert_reduce_fusion
  9.7 4.3 %fusion.28 = (s32[384]{0:T(512)S(1)}, s32[384,1]{0,1:T(1,128)S(1)}) fusion(s32[]{:T(128)} %bitcast.30, s32[]{:T(128)} %bitcast.31, s32[]{:T(128)} %bitcast.32, s32[]{:T(128)} %bitcast.33, s32[]{:T(128)} %bitcast.34, s32[]{:T(128)} %bitcast.36, s32[]{:T(128)} %bitcast.35, s32[384]{0:T(512)S(1)} %convert_reduce_fusion), kind=kLoop, calls=%fused_computation.90 | loop fusion | flops 5760 | bytes 4636 | tf_op jit(solution)/shard_map/jit(_take)/gather | solution.py:33
  14.0 0.7 fusion.48
  14.8 0.1 compare_reduce_fusion.24
  14.9 15.7 %fusion.27 = f32[384]{0:T(512)S(1)} fusion(pred[384]{0:T(512)(128)(4,1)S(1)} %get-tuple-element.31, pred[384]{0:T(512)(128)(4,1)S(1)} %get-tuple-element.30, pred[384]{0:T(512)(128)(4,1)S(1)} %get-tuple-element.29, pred[384]{0:T(512)(128)(4,1)S(1)} %get-tuple-element.28, pred[384]{0:T(512)(128)(4,1)S(1)} %get-tuple-element.27, ...), kind=kLoop, calls=%fused_computation.87 | loop fusion | flops 13056 | bytes 14308 | tf_op jit(solution)/shard_map/convert_element_type | solution.py:16
  30.6 0.1 multiply_cosine_fusion.1
  30.8 0.8 multiply_cosine_fusion
  31.5 20.0 %all-gather.3.cloned.1.call-done = bf16[384,4096]{1,0:T(8,128)(2,1)} async-done(((bf16[384,1024]{1,0:T(8,128)(2,1)}), bf16[384,4096]{1,0:T(8,128)(2,1)}) %all-gather.3.cloned.1.call-update) | async-done | bytes 3145744 | tf_op jit(solution)/shard_map/all_gather | solution.py:85
  51.6 2.7 %multiply_reduce_fusion = f32[384]{0:T(512)S(1)} fusion(bf16[384,4096]{1,0:T(8,128)(2,1)} %all-gather.3.cloned.1.call-done), kind=kLoop, calls=%fused_computation.4 | loop fusion | flops 4718208 | bytes 3147264 | tf_op jit(solution)/shard_map/reduce_sum | solution.py:89
  54.3 0.1 copy-done.1
  54.4 1.1 multiply_convert_fusion
  55.5 1.7 copy-done.2
  57.2 2.0 convolution_convert_fusion.1
  59.2 3.2 %gather_fusion.1 = bf16[32,4096]{1,0:T(8,128)(2,1)S(1)} fusion(bf16[384,4096]{1,0:T(8,128)(2,1)} %copy-done.2, s32[1024]{0:T(1024)S(1)} %pad_clamp_fusion), kind=kCustom, calls=%fused_computation.1 | custom fusion | bytes 524416 | tf_op jit(solution)/shard_map/jit(_take)/gather | solution.py:35
  62.4 4.7 %fusion.53 = f32[384,256]{0,1:T(8,128)} fusion(bf16[384,4096]{1,0:T(8,128)(2,1)} %copy-done.2, bf16[4096,256]{1,0:T(8,128)(2,1)} %param.17), kind=kOutput, calls=%fused_computation.112 | convolution fusion | flops 805306368 | bytes 5636096 | tf_op jit(solution)/shard_map/dot_general | solution.py:39
  67.2 0.9 fusion.6
  68.1 0.1 subtract_convert_fusion.1
  68.2 1.1 fusion.47
  69.3 0.2 copy.38
  69.4 0.2 copy.37
  69.6 0.8 subtract_convert_fusion
  70.4 1.4 fusion.50
  71.8 1.5 fusion.5
  73.4 3.8 %fusion.54 = f32[32,4096]{1,0:T(8,128)} fusion(bf16[32,512]{1,0:T(8,128)(2,1)S(1)} %reshape.233, bf16[512,4096]{1,0:T(8,128)(2,1)} %param.19), kind=kOutput, calls=%fused_computation.113 | convolution fusion | flops 134217728 | bytes 4751360 | tf_op jit(solution)/shard_map/dot_general | solution.py:99
  77.2 0.0 reduce-scatter.2.cloned.1.call-update
  77.2 0.0 all-gather.5.cloned.1.call-start
  77.3 0.3 fusion.24
  77.6 0.1 multiply_reduce_fusion.2
  77.7 0.1 select_reduce_fusion
  77.8 5.3 %convert_element_type.45 = f32[384,4096]{1,0:T(8,128)} convert(bf16[384,4096]{1,0:T(8,128)(2,1)} %all-gather.3.cloned.1.call-done) | non-fusion elementwise | flops 1572864 | bytes 9437184 | tf_op jit(solution)/shard_map/convert_element_type | solution.py:86
  83.1 3.8 %gather_fusion = f32[32,4096]{1,0:T(8,128)S(1)} fusion(f32[384,4096]{1,0:T(8,128)} %convert_element_type.45, s32[1024]{0:T(1024)S(1)} %pad_clamp_fusion), kind=kCustom, calls=%fused_computation | custom fusion | bytes 1048704 | tf_op jit(solution)/shard_map/jit(_take)/gather | solution.py:93
  86.9 10.1 %reduce-scatter.2.cloned.1.call-done = f32[32,1024]{1,0:T(8,128)} async-done(((f32[32,4096]{1,0:T(8,128)}), f32[32,1024]{1,0:T(8,128)}) %reduce-scatter.2.cloned.1.call-update) | async-done | bytes 131088 | tf_op jit(solution)/shard_map/reduce_scatter | solution.py:100
  96.9 1.1 multiply_reduce_fusion.3
  98.0 7.1 %all-reduce = (f32[32]{0:T(128)S(1)}, f32[32]{0:T(128)S(1)}) all-reduce(f32[32]{0:T(128)S(1)} %multiply_reduce_fusion.2, f32[32]{0:T(128)S(1)} %multiply_reduce_fusion.3), channel_id=1, replica_groups=mesh['corpus'=32,'tensor'=4] {'tensor'}, use_global_device_ids=true, to_apply=%region_10.11 | all-reduce | flops 64 | bytes 512 | tf_op jit(solution)/shard_map/psum | solution.py:106
  105.1 1.1 multiply_reduce_fusion.1
  106.2 6.4 %psum.23 = f32[32]{0:T(128)S(1)} all-reduce(f32[32]{0:T(128)S(1)} %get-tuple-element.34), channel_id=1, replica_groups=mesh['corpus'=32,'tensor'=4] {'tensor'}, use_global_device_ids=true, to_apply=%region_12.13 | all-reduce | flops 32 | bytes 256 | tf_op jit(solution)/shard_map/psum | solution.py:111
  112.6 0.1 multiply_convert_fusion.1
  112.7 10.3 %all_gather.10 = bf16[32,4096]{1,0:T(8,128)(2,1)} all-gather(bf16[32,1024]{1,0:T(8,128)(2,1)S(1)} %multiply_convert_fusion.1), channel_id=1, replica_groups=mesh['corpus'=32,'tensor'=4] {'tensor'}, dimensions={1}, use_global_device_ids=true | all-gather | bytes 327680 | tf_op jit(solution)/shard_map/all_gather | solution.py:113
  123.0 0.0 all-gather.5.cloned.1.call-update
  123.0 62.5 %all-gather.5.cloned.1.call-done = bf16[1024,4096]{1,0:T(8,128)(2,1)} async-done(((bf16[32,4096]{1,0:T(8,128)(2,1)}), bf16[1024,4096]{1,0:T(8,128)(2,1)}) %all-gather.5.cloned.1.call-update) | async-done | bytes 8388624 | tf_op jit(solution)/shard_map/all_gather | solution.py:115
  185.5 14.7 %convolution_convert_fusion = bf16[1024,1024]{1,0:T(8,128)(2,1)} fusion(bf16[1024,4096]{1,0:T(8,128)(2,1)} %all-gather.5.cloned.1.call-done, bf16[1024,4096]{1,0:T(8,128)(2,1)} %param.23), kind=kOutput, calls=%fused_computation.5 | convolution fusion | flops 8590983168 | bytes 18874368 | tf_op jit(solution)/shard_map/dot_general | solution.py:114
  (33 shorter events, 0.2 us)
Async XLA Ops:
  6.5 50.6 %copy-start = (bf16[4096,256]{1,0:T(8,128)(2,1)S(1)}, bf16[4096,256]{1,0:T(8,128)(2,1)}, u32[]{:S(2)}) copy-start(bf16[4096,256]{1,0:T(8,128)(2,1)} %param.18) | copy-start | bytes 6291460
  6.5 47.8 %copy-start.5 = (f32[4096]{0:T(1024)S(1)}, f32[4096]{0:T(1024)}, u32[]{:S(2)}) copy-start(f32[4096]{0:T(1024)} %param.15) | copy-start | bytes 49156
  6.5 45.0 %all-gather.3.cloned.1.call-start = ((), (), s32[]{:S(2)}) async-start(), calls=%async_computation.1 | async-start | bytes 3932160 | tf_op jit(solution)/shard_map/all_gather | solution.py:85
  7.3 89.7 %reduce-scatter.2.cloned.1.call-start = ((), (), s32[]{:S(2)}) async-start(), calls=%async_computation.2 | async-start | bytes 655360 | tf_op jit(solution)/shard_map/reduce_scatter | solution.py:100
  14.9 52.3 %copy-start.6 = (pred[32]{0:T(512)(128)(4,1)}, pred[32]{0:T(512)(128)(4,1)S(1)}, u32[]{:S(2)}) copy-start(pred[32]{0:T(512)(128)(4,1)S(1)} %compare_and_fusion) | copy-start | bytes 100
  51.6 2.8 %copy-start.1 = (bf16[384,4096]{1,0:T(8,128)(2,1)S(1)}, bf16[384,4096]{1,0:T(8,128)(2,1)}, u32[]{:S(2)}) copy-start(bf16[384,4096]{1,0:T(8,128)(2,1)} %all-gather.3.cloned.1.call-done) | copy-start | bytes 9437188
  55.5 1.7 copy-start.2
  62.4 4.7 %copy-start.3 = (bf16[4096,512]{1,0:T(8,128)(2,1)S(1)}, bf16[4096,512]{1,0:T(8,128)(2,1)}, u32[]{:S(2)}) copy-start(bf16[4096,512]{1,0:T(8,128)(2,1)} %param.16) | copy-start | bytes 12582916
  70.4 6.9 %copy-start.4 = (bf16[16,4096]{1,0:T(8,128)(2,1)S(1)}, bf16[16,4096]{1,0:T(8,128)(2,1)}, u32[]{:S(2)}) copy-start(bf16[16,4096]{1,0:T(8,128)(2,1)} %param.20) | copy-start | bytes 393220
  70.4 6.9 %copy-start.8 = (s32[32]{0:T(128)S(1)}, s32[32]{0:T(128)}, u32[]{:S(2)}) copy-start(s32[32]{0:T(128)} %param.14) | copy-start | bytes 388
  70.4 7.3 %copy-start.9 = (f32[16]{0:T(128)S(1)}, f32[16]{0:T(128)}, u32[]{:S(2)}) copy-start(f32[16]{0:T(128)} %param.21) | copy-start | bytes 196
  77.2 108.3 %all-gather.5.cloned.1.call-start = ((), (), s32[]{:S(2)}) async-start(), calls=%async_computation.3 | async-start | bytes 8650752 | tf_op jit(solution)/shard_map/all_gather | solution.py:115
  83.1 13.8 %copy-start.7 = (pred[32]{0:T(512)(128)(4,1)S(1)}, pred[32]{0:T(512)(128)(4,1)}, u32[]{:S(2)}) copy-start(pred[32]{0:T(512)(128)(4,1)} %copy-done.6) | copy-start | bytes 100
  83.1 22.0 %dynamic-slice-start = ((f32[4096]{0:T(1024)}, s32[]{:T(128)}), f32[1024]{0:T(1024)S(1)}, s32[]{:S(2)}) async-start(f32[4096]{0:T(1024)} %param.22, s32[]{:T(128)} %select_n.69), calls=%async_computation.4 | async-start | bytes 8704 | tf_op jit(solution)/shard_map/dynamic_slice | solution.py:105
Sparse Core Ops, SparseCore 0:
  9.0 42.5 all-gather.2
  77.4 19.5 reduce-scatter.1
  123.2 62.3 all-gather.4
where the time goes:
time: 207 us
  waiting for transfers between devices  93.3 us (45%)
  other arithmetic  34.6 us (17%)
  matrix products  29.3 us (14%)
  blocking collectives  23.7 us (11%)
  between operations  13.3 us (6%)
  local copies, waits for them, and re-layouts  12.4 us (6%)
    all_gather x1, waiting for transfers between devices, on_device(): lax.all_gather(embeddings, 'corpus', axis=0, tiled=True)  62.5 us
    all_gather x1, waiting for transfers between devices, on_device(): group_rows = lax.all_gather(hidden, 'tensor', axis=1, tiled=True)  20 us
    convert_element_type x2, other arithmetic, rotate(): angles = positions.astype(jnp.float32)[:, None] * frequency[None, :]  16.4 us
    dot_general x1, matrix products, on_device(): lax.dot_general(lax.all_gather(embeddings, 'corpus', axis=0, tiled=True),...  14.7 us
    all_gather x1, blocking collectives, on_device(): embeddings = lax.all_gather(local_embed, 'tensor', axis=1, tiled=True)  10.3 us
    reduce_scatter x1, waiting for transfers between devices, on_device(): lax.psum_scatter(partial_value, 'tensor', scatter_dimension=1, tiled=True)  10.1 us
    psum x1, blocking collectives, on_device(): lax.psum((jnp.sum(residual * residual, axis=1), jnp.sum(my_steering * my_...  7.05 us
    psum x1, blocking collectives, on_device(): totals = lax.psum(jnp.sum(gained * gained, axis=1), 'tensor')  6.39 us
  transfers between devices with their start and end apart: 3, of which 3 were waited for; matrix products, arithmetic and copies ran while one was open for 16% of the time, Pallas kernels for 0%

commit v1 on v0

--- a/solution.py
+++ b/solution.py
@@ -2,10 +2,14 @@
 import jax.numpy as jnp
 from jax import lax
 from jax.sharding import PartitionSpec as P
+from jax.lax import all_to_all, axis_size
 
 D = 4096
 HEAD = 128
 rope_base = 1000000.0
+press_edge = lambda x_local: jnp.concatenate(
+    all_to_all(jnp.stack([x_local for _ in range(axis_size("corpus"))]), "corpus", 0, 0), axis=0
+)
 
 
 def rotate(vectors, positions):
@@ -112,7 +116,7 @@
     local_embed = (gained * lax.rsqrt(totals + 1e-06)[:, None]).astype(jnp.bfloat16)
     embeddings = lax.all_gather(local_embed, "tensor", axis=1, tiled=True)
     return lax.dot_general(
-        lax.all_gather(embeddings, "corpus", axis=0, tiled=True),
+        press_edge(embeddings),
         index_rows,
         (((1,), (1,)), ((), ())),
         preferred_element_type=jnp.float32,

time: 207 us -> 255 us (1.23)
  blocking collectives: 23.7 us -> 135 us
  waiting for transfers between devices: 93.3 us -> 30.8 us
    all_to_all x0 -> x1, blocking collectives: none -> 112 us  [all_to_all(jnp.stack([x_local for _ in range(axis_size('corpus'))]), 'cor...]
    all_gather x1 -> x0, waiting for transfers between devices: 62.5 us -> none  [on_device(): lax.all_gather(embeddings, 'corpus', axis=0, tiled=True)]
  transfers between devices with their start and end apart: 3 -> 2, of which waited for: 3 -> 2; matrix products, arithmetic and copies ran while one was open for 16% -> 13% of each run, Pallas kernels for 0% -> 0%
where the time goes in v1:
time: 255 us
  blocking collectives  135 us (53%)
  other arithmetic  34.6 us (14%)
  waiting for transfers between devices  30.8 us (12%)
  matrix products  26.8 us (11%)
  between operations  13.6 us (5%)
  local copies, waits for them, and re-layouts  13.5 us (5%)
    all_to_all x1, blocking collectives, all_to_all(jnp.stack([x_local for _ in range(axis_size('corpus'))]), 'cor...  112 us
    all_gather x1, waiting for transfers between devices, on_device(): group_rows = lax.all_gather(hidden, 'tensor', axis=1, tiled=True)  20 us
    convert_element_type x2, other arithmetic, rotate(): angles = positions.astype(jnp.float32)[:, None] * frequency[None, :]  16.4 us
    dot_general x1, matrix products, on_device(): lax.dot_general(press_edge(embeddings), index_rows, (((1,), (1,)), ((), (...  12.2 us
    reduce_scatter x1, waiting for transfers between devices, on_device(): lax.psum_scatter(partial_value, 'tensor', scatter_dimension=1, tiled=True)  10.1 us
    all_gather x1, blocking collectives, on_device(): embeddings = lax.all_gather(local_embed, 'tensor', axis=1, tiled=True)  9.36 us
    psum x1, blocking collectives, on_device(): lax.psum((jnp.sum(residual * residual, axis=1), jnp.sum(my_steering * my_...  7.05 us
    psum x1, blocking collectives, on_device(): totals = lax.psum(jnp.sum(gained * gained, axis=1), 'tensor')  6.39 us
  transfers between devices with their start and end apart: 2, of which 2 were waited for; matrix products, arithmetic and copies ran while one was open for 13% of the time, Pallas kernels for 0%

profile of v1, /device:TPU:1, one launch (start us, length us, event | category | flops | bytes accessed | tf_op | source)
XLA Modules:
  0.0 254.6 jit_solution(16187978500825321272)
XLA Ops:
  6.5 0.7 all-gather.2.cloned.1.call-update
  7.3 0.0 reduce-scatter.2.cloned.1.call-start
  7.3 0.7 copy.26
  8.0 0.1 reduce-window.4
  8.1 0.1 fusion.23
  8.2 0.7 fusion.29
  8.9 0.7 fusion.49
  9.6 0.1 convert_reduce_fusion
  9.7 4.3 %fusion.28 = (s32[384]{0:T(512)S(1)}, s32[384,1]{0,1:T(1,128)S(1)}) fusion(s32[]{:T(128)} %bitcast.30, s32[]{:T(128)} %bitcast.31, s32[]{:T(128)} %bitcast.32, s32[]{:T(128)} %bitcast.33, s32[]{:T(128)} %bitcast.34, s32[]{:T(128)} %bitcast.36, s32[]{:T(128)} %bitcast.35, s32[384]{0:T(512)S(1)} %convert_reduce_fusion), kind=kLoop, calls=%fused_computation.90 | loop fusion | flops 5760 | bytes 4636 | tf_op jit(solution)/shard_map/jit(_take)/gather | solution.py:37
  14.0 0.7 fusion.48
  14.8 0.1 compare_reduce_fusion.24
  14.9 15.7 %fusion.27 = f32[384]{0:T(512)S(1)} fusion(pred[384]{0:T(512)(128)(4,1)S(1)} %get-tuple-element.31, pred[384]{0:T(512)(128)(4,1)S(1)} %get-tuple-element.30, pred[384]{0:T(512)(128)(4,1)S(1)} %get-tuple-element.29, pred[384]{0:T(512)(128)(4,1)S(1)} %get-tuple-element.28, pred[384]{0:T(512)(128)(4,1)S(1)} %get-tuple-element.27, ...), kind=kLoop, calls=%fused_computation.87 | loop fusion | flops 13056 | bytes 14308 | tf_op jit(solution)/shard_map/convert_element_type | solution.py:20
  30.6 0.1 multiply_cosine_fusion.1
  30.8 0.8 multiply_cosine_fusion
  31.5 20.0 %all-gather.2.cloned.1.call-done = bf16[384,4096]{1,0:T(8,128)(2,1)} async-done(((bf16[384,1024]{1,0:T(8,128)(2,1)}), bf16[384,4096]{1,0:T(8,128)(2,1)}) %all-gather.2.cloned.1.call-update) | async-done | bytes 3145744 | tf_op jit(solution)/shard_map/all_gather | solution.py:89
  51.6 2.7 %multiply_reduce_fusion = f32[384]{0:T(512)S(1)} fusion(bf16[384,4096]{1,0:T(8,128)(2,1)} %all-gather.2.cloned.1.call-done), kind=kLoop, calls=%fused_computation.4 | loop fusion | flops 4718208 | bytes 3147264 | tf_op jit(solution)/shard_map/reduce_sum | solution.py:93
  54.3 0.1 copy-done.1
  54.4 1.1 multiply_convert_fusion
  55.5 1.7 copy-done.2
  57.2 2.0 convolution_convert_fusion.1
  59.2 3.2 %gather_fusion.1 = bf16[32,4096]{1,0:T(8,128)(2,1)S(1)} fusion(bf16[384,4096]{1,0:T(8,128)(2,1)} %copy-done.2, s32[1024]{0:T(1024)S(1)} %pad_clamp_fusion), kind=kCustom, calls=%fused_computation.1 | custom fusion | bytes 524416 | tf_op jit(solution)/shard_map/jit(_take)/gather | solution.py:39
  62.4 0.0 copy-start.3
  62.4 4.7 %fusion.53 = f32[384,256]{0,1:T(8,128)} fusion(bf16[384,4096]{1,0:T(8,128)(2,1)} %copy-done.2, bf16[4096,256]{1,0:T(8,128)(2,1)} %param.17), kind=kOutput, calls=%fused_computation.112 | convolution fusion | flops 805306368 | bytes 5636096 | tf_op jit(solution)/shard_map/dot_general | solution.py:43
  67.2 0.9 fusion.6
  68.1 0.1 subtract_convert_fusion.1
  68.2 1.1 fusion.47
  69.3 0.2 copy.38
  69.4 0.2 copy.37
  69.6 0.8 subtract_convert_fusion
  70.4 1.4 fusion.50
  71.8 1.5 fusion.5
  73.4 3.8 %fusion.54 = f32[32,4096]{1,0:T(8,128)} fusion(bf16[32,512]{1,0:T(8,128)(2,1)S(1)} %reshape.238, bf16[512,4096]{1,0:T(8,128)(2,1)} %param.19), kind=kOutput, calls=%fused_computation.113 | convolution fusion | flops 134217728 | bytes 4751360 | tf_op jit(solution)/shard_map/dot_general | solution.py:103
  77.2 0.0 reduce-scatter.2.cloned.1.call-update
  77.3 0.3 fusion.24
  77.5 0.1 multiply_reduce_fusion.2
  77.7 0.1 select_reduce_fusion
  77.8 5.3 %convert_element_type.45 = f32[384,4096]{1,0:T(8,128)} convert(bf16[384,4096]{1,0:T(8,128)(2,1)} %all-gather.2.cloned.1.call-done) | non-fusion elementwise | flops 1572864 | bytes 9437184 | tf_op jit(solution)/shard_map/convert_element_type | solution.py:90
  83.1 3.8 %gather_fusion = f32[32,4096]{1,0:T(8,128)S(1)} fusion(f32[384,4096]{1,0:T(8,128)} %convert_element_type.45, s32[1024]{0:T(1024)S(1)} %pad_clamp_fusion), kind=kCustom, calls=%fused_computation | custom fusion | bytes 1048704 | tf_op jit(solution)/shard_map/jit(_take)/gather | solution.py:97
  86.8 10.1 %reduce-scatter.2.cloned.1.call-done = f32[32,1024]{1,0:T(8,128)} async-done(((f32[32,4096]{1,0:T(8,128)}), f32[32,1024]{1,0:T(8,128)}) %reduce-scatter.2.cloned.1.call-update) | async-done | bytes 131088 | tf_op jit(solution)/shard_map/reduce_scatter | solution.py:104
  96.9 1.1 multiply_reduce_fusion.3
  98.0 7.1 %all-reduce = (f32[32]{0:T(128)S(1)}, f32[32]{0:T(128)S(1)}) all-reduce(f32[32]{0:T(128)S(1)} %multiply_reduce_fusion.2, f32[32]{0:T(128)S(1)} %multiply_reduce_fusion.3), channel_id=1, replica_groups=mesh['corpus'=32,'tensor'=4] {'tensor'}, use_global_device_ids=true, to_apply=%region_10.11 | all-reduce | flops 64 | bytes 512 | tf_op jit(solution)/shard_map/psum | solution.py:110
  105.1 1.1 multiply_reduce_fusion.1
  106.2 6.4 %psum.23 = f32[32]{0:T(128)S(1)} all-reduce(f32[32]{0:T(128)S(1)} %get-tuple-element.34), channel_id=1, replica_groups=mesh['corpus'=32,'tensor'=4] {'tensor'}, use_global_device_ids=true, to_apply=%region_12.13 | all-reduce | flops 32 | bytes 256 | tf_op jit(solution)/shard_map/psum | solution.py:115
  112.6 0.1 multiply_convert_fusion.1
  112.7 9.4 %all_gather.7 = bf16[32,4096]{1,0:T(8,128)(2,1)S(1)} all-gather(bf16[32,1024]{1,0:T(8,128)(2,1)S(1)} %multiply_convert_fusion.1), channel_id=1, replica_groups=mesh['corpus'=32,'tensor'=4] {'tensor'}, dimensions={1}, use_global_device_ids=true | all-gather | bytes 327680 | tf_op jit(solution)/shard_map/all_gather | solution.py:117
  122.1 1.0 stack.2
  123.1 112.4 %all_to_all.5 = bf16[32,32,4096]{2,1,0:T(8,128)(2,1)S(1)} all-to-all(bf16[32,32,4096]{2,1,0:T(8,128)(2,1)S(1)} %stack.2), channel_id=1, replica_groups=mesh['corpus'=32,'tensor'=4] {'corpus'}, dimensions={0} | all-to-all | bytes 16777216 | tf_op jit(solution)/shard_map/all_to_all | solution.py:11
  235.5 12.2 %convolution_convert_fusion = bf16[1024,1024]{1,0:T(8,128)(2,1)} fusion(bf16[1024,4096]{1,0:T(8,128)(2,1)S(1)} %bitcast.89, bf16[1024,4096]{1,0:T(8,128)(2,1)} %param.23), kind=kOutput, calls=%fused_computation.5 | convolution fusion | flops 8590983168 | bytes 18874368 | tf_op jit(solution)/shard_map/dot_general | solution.py:118
  (32 shorter events, 0.2 us)
Async XLA Ops:
  6.5 50.6 %copy-start = (bf16[4096,256]{1,0:T(8,128)(2,1)S(1)}, bf16[4096,256]{1,0:T(8,128)(2,1)}, u32[]{:S(2)}) copy-start(bf16[4096,256]{1,0:T(8,128)(2,1)} %param.18) | copy-start | bytes 6291460
  6.5 47.8 %copy-start.5 = (f32[4096]{0:T(1024)S(1)}, f32[4096]{0:T(1024)}, u32[]{:S(2)}) copy-start(f32[4096]{0:T(1024)} %param.15) | copy-start | bytes 49156
  6.5 45.0 %all-gather.2.cloned.1.call-start = ((), (), s32[]{:S(2)}) async-start(), calls=%async_computation.2 | async-start | bytes 3932160 | tf_op jit(solution)/shard_map/all_gather | solution.py:89
  7.3 89.7 %reduce-scatter.2.cloned.1.call-start = ((), (), s32[]{:S(2)}) async-start(), calls=%async_computation.3 | async-start | bytes 655360 | tf_op jit(solution)/shard_map/reduce_scatter | solution.py:104
  14.9 52.3 %copy-start.6 = (pred[32]{0:T(512)(128)(4,1)}, pred[32]{0:T(512)(128)(4,1)S(1)}, u32[]{:S(2)}) copy-start(pred[32]{0:T(512)(128)(4,1)S(1)} %compare_and_fusion) | copy-start | bytes 100
  51.6 2.8 %copy-start.1 = (bf16[384,4096]{1,0:T(8,128)(2,1)S(1)}, bf16[384,4096]{1,0:T(8,128)(2,1)}, u32[]{:S(2)}) copy-start(bf16[384,4096]{1,0:T(8,128)(2,1)} %all-gather.2.cloned.1.call-done) | copy-start | bytes 9437188
  55.5 1.7 copy-start.2
  62.4 4.7 %copy-start.3 = (bf16[4096,512]{1,0:T(8,128)(2,1)S(1)}, bf16[4096,512]{1,0:T(8,128)(2,1)}, u32[]{:S(2)}) copy-start(bf16[4096,512]{1,0:T(8,128)(2,1)} %param.16) | copy-start | bytes 12582916
  70.4 6.9 %copy-start.4 = (bf16[16,4096]{1,0:T(8,128)(2,1)S(1)}, bf16[16,4096]{1,0:T(8,128)(2,1)}, u32[]{:S(2)}) copy-start(bf16[16,4096]{1,0:T(8,128)(2,1)} %param.20) | copy-start | bytes 393220
  70.4 6.9 %copy-start.8 = (s32[32]{0:T(128)S(1)}, s32[32]{0:T(128)}, u32[]{:S(2)}) copy-start(s32[32]{0:T(128)} %param.14) | copy-start | bytes 388
  70.4 7.3 %copy-start.9 = (f32[16]{0:T(128)S(1)}, f32[16]{0:T(128)}, u32[]{:S(2)}) copy-start(f32[16]{0:T(128)} %param.21) | copy-start | bytes 196
  83.1 13.9 %copy-start.7 = (pred[32]{0:T(512)(128)(4,1)S(1)}, pred[32]{0:T(512)(128)(4,1)}, u32[]{:S(2)}) copy-start(pred[32]{0:T(512)(128)(4,1)} %copy-done.6) | copy-start | bytes 100
  83.1 22.0 %dynamic-slice-start = ((f32[4096]{0:T(1024)}, s32[]{:T(128)}), f32[1024]{0:T(1024)S(1)}, s32[]{:S(2)}) async-start(f32[4096]{0:T(1024)} %param.22, s32[]{:T(128)} %select_n.69), calls=%async_computation.4 | async-start | bytes 8704 | tf_op jit(solution)/shard_map/dynamic_slice | solution.py:109
Sparse Core Ops, SparseCore 0:
  9.0 42.5 all-gather.1
  77.4 19.5 reduce-scatter.1
